TPU v7x, 32 devices: a whole 2x2x4 slice. The times are simulated.
32 devices in a mesh: pat: 8 (over y, x, core), feat: 4 (over z).
Axes of the slice: x: 2, y: 2, z: 4, core: 2. Of those that a mesh axis runs over, the one named last changes fastest.
Arguments:
- visits: bfloat16 [32768, 8192], P('pat', 'feat'), may hold values from -1.5 to 1.5
- counts: int32 [64], P('pat'), may hold values from 128 to 512, as said below
- patient_weight: float32 [64, 128], P('pat'), may hold values from 0.5 to 2
- phenotype_core: float32 [128, 128], replicated, may hold values from -0.5 to 0.5
- feature_factor: bfloat16 [8192, 128], P('feat'), may hold values from -0.0625 to 0.0625
- static_data: bfloat16 [64, 4096], P('pat', 'feat'), may hold values from -6 to 6
- static_factor: bfloat16 [4096, 128], P('feat'), may hold values from -0.09375 to 0.09375
Outputs:
- core_new: float32 [128, 128], replicated
- feature_new: float32 [8192, 128], P('feat')
- patient_new: float32 [64, 128], P('pat')
- static_new: float32 [4096, 128], P('feat')
Inputs may be any that keep to these rules, and one draw needn't show every extreme that they name: `counts`: some patient of the last index of pat has exactly 512 visits.
All inputs are finite; a program needn't handle non-finite values.
Results may differ from a plain program's by a relative error of at most 0.0035.
Values may be sent and summed in bfloat16 or wider, within the bound.
A program may use at most 64 MiB of HBM per device.

v0:
```python
import functools

import jax
import jax.numpy as jnp
from jax import lax
from jax.experimental import pallas as pl
from jax.experimental.pallas import tpu as pltpu
from jax.sharding import PartitionSpec as P

BLK = 128
NS_STEPS = 8
MU_RIDGE = 1.0
F32 = jnp.float32
BF16 = jnp.bfloat16
MESH = pl.DeviceIdType.MESH

NN = (((1,), (0,)), ((), ()))
NT = (((1,), (1,)), ((), ()))
TN = (((0,), (0,)), ((), ()))


def dg(a, b, dims):
    return lax.dot_general(a, b, dims, preferred_element_type=F32)


def split(x):
    hi = x.astype(BF16)
    return hi, (x - hi.astype(F32)).astype(BF16)


def dot3(a, b, dims=NN):
    a_hi, a_lo = split(a)
    b_hi, b_lo = split(b)
    return dg(a_hi, b_hi, dims) + (dg(a_hi, b_lo, dims) + dg(a_lo, b_hi, dims))


def exact(a, b, dims=NN):
    return lax.dot_general(
        a, b, dims, precision=lax.Precision.HIGHEST, preferred_element_type=F32
    )


def solve(rhs, matrix, inverse):
    guess = dot3(rhs, inverse)
    return guess + dot3(rhs - exact(guess, matrix), inverse)


def kernel(
    n_pat, n_feat, chunks, tiles,
    counts, visits, weight, core, factor_in, static_data, static_factor,
    core_new, feature_new, patient_new, static_new,
    vis, proj, part, low_in, high_in, total,
    gram_out, gram_low, gram_high, gram_total, weights_all, static_all,
    mats, inverses, wides, row_weights, squares, grams, factors, halves, updates,
    terms_out, terms_in, core_out, core_in, new_out, new_in, coreg_out, coreg_in,
    vis_sem, part_send, low_recv, high_recv, total_send, total_recv,
    gram_sem, weight_send, weight_recv, static_send, static_recv,
    terms_send, terms_recv, core_send, core_recv,
    new_send, new_recv, coreg_send, coreg_recv,
):
    me = lax.axis_index("pat")
    z = lax.axis_index("feat")
    rank = core.shape[0]
    rows = visits.shape[0]
    rows_chunk = rows // chunks
    patients = weight.shape[0]
    features = visits.shape[1]
    piece = features // n_pat
    owners, core_rows = core_out.shape[0], core_out.shape[1]
    inner = z > 0
    outer = z < n_feat - 1

    def remote(src, dst, send, recv, **where):
        return pltpu.make_async_remote_copy(
            src_ref=src, dst_ref=dst, send_sem=send, recv_sem=recv,
            device_id=where, device_id_type=MESH,
        )

    def span(c):
        return pl.ds(pl.multiple_of(c * rows_chunk, rows_chunk), rows_chunk)

    def load(c):
        return pltpu.make_async_copy(visits.at[span(c)], vis.at[span(c)], vis_sem.at[c])

    @pl.loop(0, chunks)
    def _(c):
        load(c).start()

    barrier = pltpu.get_barrier_semaphore()
    for d in range(1, n_pat):
        pl.semaphore_signal(
            barrier, inc=1, device_id={"pat": lax.rem(me + d, n_pat)}, device_id_type=MESH
        )

    @pl.when(inner)
    def _():
        pl.semaphore_signal(barrier, inc=1, device_id={"feat": z - 1}, device_id_type=MESH)

    @pl.when(outer)
    def _():
        pl.semaphore_signal(barrier, inc=1, device_id={"feat": z + 1}, device_id_type=MESH)

    weights_all[me] = weight[...]
    static_all[me] = static_data[...].astype(F32)
    gram_own = jnp.concatenate(
        [
            dg(factor_in[...], factor_in[...], TN),
            dg(static_factor[...], static_factor[...], TN),
            dg(static_data[...], static_factor[...], NN),
        ],
        axis=0,
    )
    gram_out[...] = gram_own

    pl.semaphore_wait(
        barrier, n_pat - 1 + jnp.where(inner, 1, 0) + jnp.where(outer, 1, 0)
    )

    def gram_part(up):
        if up:
            return remote(gram_out, gram_low, gram_sem.at[0], gram_sem.at[1], feat=z + 1)
        return remote(gram_out, gram_high, gram_sem.at[0], gram_sem.at[2], feat=z - 1)

    def gram_back(up):
        return remote(
            gram_total, gram_total, gram_sem.at[4 if up else 3], gram_sem.at[5],
            feat=z + 1 if up else z - 1,
        )

    gram_owner = n_feat // 2

    @pl.when(z == 0)
    def _():
        gram_part(True).start()

    @pl.when(z == n_feat - 1)
    def _():
        gram_part(False).start()

    def weight_copy(d):
        peer = lax.rem(me + d, n_pat)
        return remote(
            weights_all.at[me], weights_all.at[me], weight_send.at[d], weight_recv.at[me], pat=peer
        )

    def static_copy(d):
        peer = lax.rem(me + d, n_pat)
        return remote(
            static_all.at[me], static_all.at[me], static_send.at[d], static_recv.at[me], pat=peer
        )

    for d in range(1, n_pat):
        weight_copy(d).start()
        static_copy(d).start()

    def owner_of(c):
        return n_feat // 2 - 1 + lax.rem(c, 2)

    def part_copy(c, up):
        if up:
            return remote(
                part.at[span(c)], low_in.at[span(c)], part_send.at[c], low_recv.at[c], feat=z + 1
            )
        return remote(
            part.at[span(c)], high_in.at[span(c)], part_send.at[c], high_recv.at[c], feat=z - 1
        )

    def total_copy(c, up):
        return remote(
            total.at[span(c)], total.at[span(c)], total_send.at[1 if up else 0, c],
            total_recv.at[c], feat=z + 1 if up else z - 1,
        )

    @pl.loop(0, chunks)
    def _(c):
        load(c).wait()
        product = dg(vis[span(c), :], factor_in[...], NN)
        proj[span(c), :] = product

        @pl.when(z == 0)
        def _():
            part[span(c), :] = product
            part_copy(c, True).start()

        @pl.when(z == n_feat - 1)
        def _():
            part[span(c), :] = product
            part_copy(c, False).start()

    @pl.when(inner & (z < gram_owner))
    def _():
        gram_part(True).wait_recv()
        gram_out[...] += gram_low[...]
        gram_part(True).start()

    @pl.when(outer & (z > gram_owner))
    def _():
        gram_part(False).wait_recv()
        gram_out[...] += gram_high[...]
        gram_part(False).start()

    @pl.when(z == gram_owner)
    def _():
        gram_part(True).wait_recv()
        gram_part(False).wait_recv()
        gram_total[...] = gram_out[...] + gram_low[...] + gram_high[...]
        gram_back(False).start()
        gram_back(True).start()

    def relay(c):
        owner = owner_of(c)

        @pl.when(inner & (z < owner))
        def _():
            part_copy(c, True).wait_recv()
            part[span(c), :] = proj[span(c), :] + low_in[span(c), :]
            part_copy(c, True).start()

        @pl.when(outer & (z > owner))
        def _():
            part_copy(c, False).wait_recv()
            part[span(c), :] = proj[span(c), :] + high_in[span(c), :]
            part_copy(c, False).start()

        @pl.when(z == owner)
        def _():
            part_copy(c, True).wait_recv()
            part_copy(c, False).wait_recv()
            total[span(c), :] = proj[span(c), :] + low_in[span(c), :] + high_in[span(c), :]
            total_copy(c, False).start()
            total_copy(c, True).start()

    def spread(c):
        owner = owner_of(c)

        @pl.when(z < owner)
        def _():
            total_copy(c, False).wait_recv()

            @pl.when(inner)
            def _():
                total_copy(c, False).start()

        @pl.when(z > owner)
        def _():
            total_copy(c, True).wait_recv()

            @pl.when(outer)
            def _():
                total_copy(c, True).start()

    lag = 4

    @pl.loop(0, lag)
    def _(c):
        relay(c)

    @pl.when(z < gram_owner)
    def _():
        gram_back(False).wait_recv()

        @pl.when(inner)
        def _():
            gram_back(False).start()

    @pl.when(z > gram_owner)
    def _():
        gram_back(True).wait_recv()

        @pl.when(outer)
        def _():
            gram_back(True).start()

    for d in range(1, n_pat):
        peer = lax.rem(me + d, n_pat)
        remote(
            weights_all.at[peer], weights_all.at[peer], weight_send.at[d], weight_recv.at[peer],
            pat=peer,
        ).wait_recv()
        remote(
            static_all.at[peer], static_all.at[peer], static_send.at[d], static_recv.at[peer],
            pat=peer,
        ).wait_recv()

    lane = lax.broadcasted_iota(jnp.int32, (rank, rank), 1)
    sub = lax.broadcasted_iota(jnp.int32, (rank, rank), 0)
    identity = (lane == sub).astype(F32)
    all_rows = weights_all[...].reshape(n_pat * patients, rank)
    weight_gram = exact(all_rows, all_rows, TN)
    core_gram = exact(core[...], core[...], TN)
    feature_gram = gram_total[pl.ds(0, rank), :]
    static_gram = gram_total[pl.ds(rank, rank), :]
    coupled = gram_total[pl.ds(2 * rank, patients), :]
    mats[0] = feature_gram * weight_gram + MU_RIDGE * identity
    mats[1] = core_gram * weight_gram + MU_RIDGE * identity
    mats[2] = core_gram * feature_gram + static_gram + MU_RIDGE * identity
    mats[3] = weight_gram + MU_RIDGE * identity
    inverses[...] = mats[...]

    lane_row = lax.broadcasted_iota(jnp.int32, (1, rank), 1)
    sub_col = lax.broadcasted_iota(jnp.int32, (rank, 1), 0)

    def eliminate(k):
        wholes = [inverses[m] for m in range(4)]
        lines = [inverses[m, pl.ds(k, 1), :] for m in range(4)]
        swept = []
        for whole, row in zip(wholes, lines):
            pivot = jnp.sum(jnp.where(lane_row == k, row, 0.0), axis=1, keepdims=True)
            column = jnp.sum(jnp.where(lane == k, whole, 0.0), axis=1, keepdims=True)
            inverse = 1.0 / pivot
            scaled = jnp.where(lane_row == k, inverse, row * inverse)
            cleared = jnp.where((lane == k) | (sub == k), 0.0, whole)
            swept.append(cleared - jnp.where(sub_col == k, -1.0, column) * scaled)
        for m in range(4):
            inverses[m] = swept[m]

    share = rank // chunks

    def eliminate_some(c):
        @pl.loop(0, share)
        def _(j):
            eliminate(c * share + j)

    @pl.loop(lag, chunks)
    def _(c):
        relay(c)
        spread(c - lag)
        eliminate_some(c - lag)

    @pl.loop(chunks, chunks + lag)
    def _(c):
        spread(c - lag)
        eliminate_some(c - lag)

    blocks = rows // BLK
    group = 8
    starts, ends, lives = [], [], []
    position = jnp.int32(0)
    for k in range(patients):
        starts.append(position)
        lives.append(position + counts[k])
        position = position + ((counts[k] + (BLK - 1)) & (-BLK))
        ends.append(position)

    def coefficient(b, k):
        at = b * BLK
        return jnp.where((at >= starts[k]) & (at < ends[k]), 1.0, 0.0).astype(F32)

    start_row = jnp.full((1, rank), rows, jnp.int32)
    live_row = jnp.zeros((1, rank), jnp.int32)
    patient_col = lax.broadcasted_iota(jnp.int32, (patients, 1), 0)
    start_col = jnp.full((patients, 1), rows, jnp.int32)
    end_col = jnp.zeros((patients, 1), jnp.int32)
    for k in range(patients):
        start_row = jnp.where(lane_row == k, starts[k], start_row)
        live_row = jnp.where(lane_row == k, lives[k], live_row)
        start_col = jnp.where(patient_col == k, starts[k], start_col)
        end_col = jnp.where(patient_col == k, ends[k], end_col)
    weight_hi, weight_lo = split(
        jnp.concatenate([weight[...], jnp.zeros((rank - patients, rank), F32)], axis=0)
    )
    group_rows = group * BLK
    group_row = lax.broadcasted_iota(jnp.int32, (group_rows, rank), 0)

    def group_span(g):
        return pl.ds(pl.multiple_of(g * group_rows, group_rows), group_rows)

    @pl.loop(0, blocks // group)
    def _(g):
        at = group_row + g * group_rows
        live = jnp.where((at >= start_row) & (at < live_row), 1.0, 0.0).astype(BF16)
        by_row = dg(live, weight_hi, NN) + dg(live, weight_lo, NN)
        wide = total[group_span(g), :] * by_row
        row_weights[group_span(g), :] = by_row
        wides[group_span(g), :] = wide
        for i in range(group):
            one = wide[i * BLK : (i + 1) * BLK]
            squares[g * group + i] = dot3(one, one, TN)

    for k in range(patients):

        def add_blocks(g, acc, k=k):
            for i in range(group):
                b = g * group + i
                acc = acc + coefficient(b, k) * squares[b]
            return acc

        square = lax.fori_loop(0, blocks // group, add_blocks, jnp.zeros((rank, rank), F32))
        half = dot3(core[...], square)
        halves[k] = half
        gram = dot3(half, core[...], NT)
        trace = jnp.sum(jnp.sum(gram * identity, axis=1, keepdims=True), axis=0, keepdims=True)
        grams[k] = gram / trace
        factors[k] = identity / jnp.sqrt(trace)

    @pl.loop(0, NS_STEPS)
    def _(step):
        for k in range(patients):
            moment = grams[k]
            correction = 1.5 * identity - 0.5 * moment
            both = dot3(jnp.concatenate([factors[k], moment], axis=0), correction)
            factors[k] = both[:rank]
            grams[k] = dot3(correction, both[rank:])

    core_terms = jnp.zeros((rank, rank), F32)
    for k in range(patients):
        factor = factors[k]
        core_terms = core_terms + dot3(factor, halves[k], TN)
        grams[k] = dot3(core[...], dot3(factor, core[...]), TN)

    def core_copy(d):
        peer = lax.rem(me + d, n_pat)
        return remote(
            core_out.at[lax.rem(peer, owners)], core_in.at[me], core_send.at[d],
            core_recv.at[me], pat=peer,
        )

    core_out[...] = core_terms.reshape(owners, core_rows, rank)
    core_in[me] = core_out[lax.rem(me, owners)]
    for d in range(1, n_pat):
        core_copy(d).start()

    def map_group(g, sums):
        for i in range(group):
            b = g * group + i
            span_b = pl.ds(pl.multiple_of(b * BLK, BLK), BLK)
            mapper = coefficient(b, 0) * grams[0]
            for k in range(1, patients):
                mapper = mapper + coefficient(b, k) * grams[k]
            mapped = dot3(wides[span_b, :], mapper)
            products = mapped * total[span_b, :]
            updates[span_b, :] = (mapped * row_weights[span_b, :]).astype(BF16)
            at = b * BLK
            member = jnp.where((at >= start_col) & (at < end_col), 1.0, 0.0).astype(F32)
            sums = sums + member * jnp.sum(products, axis=0, keepdims=True)
        return sums

    patient_terms = lax.fori_loop(
        0, blocks // group, map_group, jnp.zeros((patients, rank), F32)
    )

    width = features // tiles
    per = n_pat // tiles

    def terms_copy(peer):
        return remote(
            terms_out.at[peer], terms_in.at[me], terms_send.at[peer], terms_recv.at[me], pat=peer
        )

    @pl.loop(0, tiles)
    def _(s):
        tile = lax.rem(lax.div(me, per) + 1 + s, tiles)
        columns = pl.ds(pl.multiple_of(tile * width, width), width)
        acc = jnp.zeros((width, rank), F32)
        for g in range(blocks // group):
            acc = acc + dg(
                vis[g * group_rows : (g + 1) * group_rows, columns],
                updates[g * group_rows : (g + 1) * group_rows, :],
                TN,
            )
        acc = solve(acc, mats[1], inverses[1]).astype(BF16)
        for j in range(per):
            peer = tile * per + j
            terms_out[peer] = acc[j * piece : (j + 1) * piece]

            @pl.when(peer != me)
            def _():
                terms_copy(peer).start()

    def each_peer(fn):
        for d in range(1, n_pat):
            fn(d, lax.rem(me + d, n_pat))

    def arrived(buffer, send, recv):
        def one(d, peer):
            remote(
                buffer.at[peer], buffer.at[peer], send.at[d], recv.at[peer], pat=peer
            ).wait_recv()

        each_peer(one)

    arrived(core_in, core_send, core_recv)
    terms_in[me] = terms_out[me]
    arrived(terms_in, terms_send, terms_recv)

    core_sum = jnp.sum(core_in[...], axis=0)
    coreg_out[...] = solve(core_sum, mats[0], inverses[0])
    terms_sum = jnp.sum(terms_in[...].astype(F32), axis=0)
    new_out[...] = terms_sum.astype(BF16)

    def new_copy(d):
        peer = lax.rem(me + d, n_pat)
        return remote(new_out, new_in.at[me], new_send.at[d], new_recv.at[me], pat=peer)

    def coreg_copy(d):
        peer = lax.rem(me + d, n_pat)
        return remote(coreg_out, coreg_in.at[me], coreg_send.at[d], coreg_recv.at[me], pat=peer)

    for d in range(1, n_pat):
        new_copy(d).start()
        coreg_copy(d).start()
    new_in[me] = new_out[...]
    coreg_in[me] = coreg_out[...]

    patient_new[...] = solve(
        patient_terms + coupled, mats[2], inverses[2]
    )
    static_terms = dot3(static_all[...].reshape(n_pat * patients, -1), all_rows, TN)
    static_new[...] = solve(static_terms, mats[3], inverses[3])

    arrived(coreg_in, coreg_send, coreg_recv)
    for q in range(owners):
        core_new[pl.ds(q * core_rows, core_rows), :] = coreg_in[q]
    arrived(new_in, new_send, new_recv)
    feature_new[...] = new_in[...].astype(F32).reshape(features, rank)

    for d in range(1, n_pat):
        weight_copy(d).wait_send()
        static_copy(d).wait_send()
        core_copy(d).wait_send()
        new_copy(d).wait_send()
        coreg_copy(d).wait_send()
        terms_copy(lax.rem(me + d, n_pat)).wait_send()

    @pl.when(z < gram_owner)
    def _():
        gram_part(True).wait_send()

        @pl.when(inner)
        def _():
            gram_back(False).wait_send()

    @pl.when(z > gram_owner)
    def _():
        gram_part(False).wait_send()

        @pl.when(outer)
        def _():
            gram_back(True).wait_send()

    @pl.when(z == gram_owner)
    def _():
        gram_back(False).wait_send()
        gram_back(True).wait_send()

    @pl.loop(0, chunks)
    def _(c):
        owner = owner_of(c)

        @pl.when(z < owner)
        def _():
            part_copy(c, True).wait_send()

            @pl.when(inner)
            def _():
                total_copy(c, False).wait_send()

        @pl.when(z > owner)
        def _():
            part_copy(c, False).wait_send()

            @pl.when(outer)
            def _():
                total_copy(c, True).wait_send()

        @pl.when(z == owner)
        def _():
            total_copy(c, False).wait_send()
            total_copy(c, True).wait_send()


def local(n_pat, n_feat, visits, counts, weight, core, factor, static_data, static_factor):
    rows, features = visits.shape
    patients, rank = weight.shape
    columns = static_data.shape[1]
    chunks = 16
    tiles = min(n_pat, features // 128)
    core_rows = max(rank // n_pat, 16)
    owners = rank // core_rows
    gram_rows = 2 * rank + patients
    piece = features // n_pat
    vmem, dma = pltpu.VMEM, pltpu.SemaphoreType.DMA
    scratch = [
        vmem((rows, features), BF16),
        vmem((rows, rank), F32),
        vmem((rows, rank), F32),
        vmem((rows, rank), F32),
        vmem((rows, rank), F32),
        vmem((rows, rank), F32),
        vmem((gram_rows, rank), F32),
        vmem((gram_rows, rank), F32),
        vmem((gram_rows, rank), F32),
        vmem((gram_rows, rank), F32),
        vmem((n_pat, patients, rank), F32),
        vmem((n_pat, patients, columns), F32),
        vmem((4, rank, rank), F32),
        vmem((4, rank, rank), F32),
        vmem((rows, rank), F32),
        vmem((rows, rank), F32),
        vmem((rows // BLK, rank, rank), F32),
        vmem((patients, rank, rank), F32),
        vmem((patients, rank, rank), F32),
        vmem((patients, rank, rank), F32),
        vmem((rows, rank), BF16),
        vmem((n_pat, piece, rank), BF16),
        vmem((n_pat, piece, rank), BF16),
        vmem((owners, core_rows, rank), F32),
        vmem((n_pat, core_rows, rank), F32),
        vmem((piece, rank), BF16),
        vmem((n_pat, piece, rank), BF16),
        vmem((core_rows, rank), F32),
        vmem((n_pat, core_rows, rank), F32),
        dma((chunks,)),
        dma((chunks,)),
        dma((chunks,)),
        dma((chunks,)),
        dma((2, chunks)),
        dma((chunks,)),
        dma((6,)),
    ] + [dma((n_pat,))] * 12
    space = pl.BlockSpec(memory_space=pltpu.VMEM)
    return pl.pallas_call(
        functools.partial(kernel, n_pat, n_feat, chunks, tiles),
        out_shape=(
            jax.ShapeDtypeStruct((rank, rank), F32),
            jax.ShapeDtypeStruct((features, rank), F32),
            jax.ShapeDtypeStruct((patients, rank), F32),
            jax.ShapeDtypeStruct((columns, rank), F32),
        ),
        in_specs=[
            pl.BlockSpec(memory_space=pltpu.SMEM),
            pl.BlockSpec(memory_space=pl.ANY),
            space, space, space, space, space,
        ],
        out_specs=(space, space, space, space),
        scratch_shapes=scratch,
        compiler_params=pltpu.CompilerParams(
            collective_id=0, has_side_effects=True, vmem_limit_bytes=62 * 1024 * 1024
        ),
        name="sweep",
    )(counts, visits, weight, core, factor, static_data, static_factor)


def solution(mesh):
    return jax.shard_map(
        functools.partial(local, mesh.shape["pat"], mesh.shape["feat"]),
        mesh=mesh,
        in_specs=(
            P("pat", "feat"),
            P("pat"),
            P("pat", None),
            P(),
            P("feat", None),
            P("pat", "feat"),
            P("feat", None),
        ),
        out_specs=(P(), P("feat", None), P("pat", None), P("feat", None)),
        check_vma=False,
    )
```

profile of v0, /device:TPU:1, one launch (start us, length us, event | category | flops | bytes accessed | tf_op | source)
XLA Modules:
  0.0 187.4 jit_solution(15842982225514511719)
XLA Ops:
  0.6 179.9 %sweep.1 = (f32[128,128]{1,0:T(8,128)}, f32[2048,128]{1,0:T(8,128)}, f32[8,128]{1,0:T(8,128)}, f32[1024,128]{1,0:T(8,128)}) custom-call(s32[8]{0:T(128)} %counts.1, bf16[4096,2048]{1,0:T(8,128)(2,1)} %visits.1, f32[8,128]{1,0:T(8,128)} %weight.1, f32[128,128]{1,0:T(8,128)} %core.1, bf16[2048,128]{1,0:T(8,128)(2,1)} %factor_in.1, ...), custom_call_target="tpu_custom_call" | custom-call | tf_op jit(solution)/shard_map/sweep/pallas_call | solution.py:622
  180.5 1.5 copy.15
  182.0 2.3 %copy.16 = f32[2048,128]{1,0:T(8,128)} copy(f32[2048,128]{1,0:T(8,128)} %get-tuple-element.9) | data formatting | bytes 2097152
  184.3 1.3 copy.17
  185.5 1.9 copy.18
where the time goes:
time: 188 us; the launch traced here: 187 us
  Pallas kernels  180 us (96%)
  local copies, waits for them, and re-layouts  6.88 us (4%)
    pallas_call x1, Pallas kernels, local(): pl.pallas_call(functools.partial(kernel, n_pat, n_feat, chunks, tiles), o...  180 us
    unnamed x4, local copies, waits for them, and re-layouts  6.88 us

commit v1 on v0

v1 whole, which is shorter than its diff:
```python
import functools

import jax
import jax.numpy as jnp
from jax import lax
from jax.experimental import pallas as pl
from jax.experimental.pallas import tpu as pltpu
from jax.sharding import PartitionSpec as P

BLK = 128
NS_STEPS = 8
MU_RIDGE = 1.0
MAXV = 512
LEVELS = 32766.0
F32 = jnp.float32
BF16 = jnp.bfloat16
MESH = pl.DeviceIdType.MESH

NN = (((1,), (0,)), ((), ()))
NT = (((1,), (1,)), ((), ()))
TN = (((0,), (0,)), ((), ()))


def dg(a, b, dims):
    return lax.dot_general(a, b, dims, preferred_element_type=F32)


def split(x):
    hi = x.astype(BF16)
    return hi, (x - hi.astype(F32)).astype(BF16)


def join(x):
    return jnp.concatenate(split(x), axis=1)


def twice(x):
    wide = join(x)
    return jnp.concatenate([wide, wide], axis=0)


def halves_sum(x):
    n = x.shape[1] // 2
    return x[:, :n] + x[:, n:]


def dot4(a, b):
    return halves_sum(dg(join(a), twice(b), NN))


def dot4_nt(a, b):
    hi, lo = split(b)
    rows = jnp.concatenate(
        [jnp.concatenate([hi, hi], axis=1), jnp.concatenate([lo, lo], axis=1)], axis=0
    )
    return halves_sum(dg(join(a), rows, NT))


def dot4_tn(a, b):
    return halves_sum(dg(jnp.concatenate(split(a), axis=0), twice(b), TN))


def exact(a, b, dims=NN):
    return lax.dot_general(
        a, b, dims, precision=lax.Precision.HIGHEST, preferred_element_type=F32
    )


def solve(rhs, matrix, inverse):
    guess = dot4(rhs, inverse)
    return guess + dot4(rhs - exact(guess, matrix), inverse)


def kernel(
    n_pat, n_feat, chunks, tiles,
    counts, visits, weight, core, factor_in, static_data, static_factor,
    core_new, feature_new, patient_new, static_new,
    vis, proj, total, codes, scales,
    gram_own, gram_parts, gram_mine, gram_all, coupled_own, coupled_parts,
    weights_all, static_all,
    mats, work, inverses, wides, row_weights, squares, grams, factors, halves, mappers, updates,
    patient_sum, patient_used, core_sum_own, core_used,
    terms_out, terms_in, core_in, new_out, new_in, coreg_out, coreg_in,
    vis_sem, line_send, line_recv,
    gram_send, gram_recv, coupled_send, coupled_recv, patient_send, patient_recv,
    core_z_send, core_z_recv, inv_send, inv_recv,
    gram_all_send, gram_all_recv, weight_send, weight_recv, static_send, static_recv,
    terms_send, terms_recv, core_send, core_recv,
    new_send, new_recv, coreg_send, coreg_recv,
):
    me = lax.axis_index("pat")
    z = lax.axis_index("feat")
    rank = core.shape[0]
    rows = visits.shape[0]
    rows_chunk = rows // chunks
    patients = weight.shape[0]
    features = visits.shape[1]
    piece = features // n_pat
    core_rows = coreg_out.shape[0]
    owners = rank // core_rows
    blocks = rows // BLK
    per_chunk = rows_chunk // BLK
    inner = z > 0
    outer = z < n_feat - 1
    lower = z < n_feat // 2
    source = n_feat // 2
    quad = 4

    def remote(src, dst, send, recv, **where):
        return pltpu.make_async_remote_copy(
            src_ref=src, dst_ref=dst, send_sem=send, recv_sem=recv,
            device_id=where, device_id_type=MESH,
        )

    def span(c):
        return pl.ds(pl.multiple_of(c * rows_chunk, rows_chunk), rows_chunk)

    def load(c):
        return pltpu.make_async_copy(visits.at[span(c)], vis.at[span(c)], vis_sem.at[c])

    def pat_peer(d):
        return lax.rem(me + d, n_pat)

    def feat_peer(d):
        return lax.rem(z + d, n_feat)

    @pl.loop(0, chunks)
    def _(c):
        load(c).start()

    barrier = pltpu.get_barrier_semaphore()
    for d in range(1, n_pat):
        pl.semaphore_signal(
            barrier, inc=1, device_id={"pat": pat_peer(d)}, device_id_type=MESH
        )
    for d in range(1, n_feat):
        pl.semaphore_signal(
            barrier, inc=1, device_id={"feat": feat_peer(d)}, device_id_type=MESH
        )

    weights_all[me] = weight[...]
    static_all[me] = static_data[...].astype(F32)
    gram_own[0] = dg(factor_in[...], factor_in[...], TN).reshape(owners, core_rows, rank)
    gram_own[1] = dg(static_factor[...], static_factor[...], TN).reshape(owners, core_rows, rank)
    coupled_own[...] = dg(static_data[...], static_factor[...], NN)
    mine = lax.rem(me, owners)
    for m in range(2):
        gram_parts[z, m] = gram_own[m, mine]
    coupled_parts[z] = coupled_own[...]

    pl.semaphore_wait(barrier, n_pat - 1 + n_feat - 1)

    def gram_copy(d):
        return remote(
            gram_parts.at[z], gram_parts.at[z], gram_send.at[d], gram_recv.at[z], feat=feat_peer(d)
        )

    def coupled_copy(d):
        return remote(
            coupled_own, coupled_parts.at[z], coupled_send.at[d], coupled_recv.at[z],
            feat=feat_peer(d),
        )

    def weight_copy(d):
        return remote(
            weights_all.at[me], weights_all.at[me], weight_send.at[d], weight_recv.at[me],
            pat=pat_peer(d),
        )

    def static_copy(d):
        return remote(
            static_all.at[me], static_all.at[me], static_send.at[d], static_recv.at[me],
            pat=pat_peer(d),
        )

    def gram_all_copy(d):
        return remote(
            gram_mine, gram_all.at[me], gram_all_send.at[d], gram_all_recv.at[me], pat=pat_peer(d)
        )

    for d in range(1, n_feat):
        gram_copy(d).start()
        coupled_copy(d).start()
    for d in range(1, n_pat):
        weight_copy(d).start()
        static_copy(d).start()

    def each_peer(fn):
        for d in range(1, n_pat):
            fn(d, pat_peer(d))

    def arrived(buffer, send, recv):
        def one(d, peer):
            remote(
                buffer.at[peer], buffer.at[peer], send.at[d], recv.at[peer], pat=peer
            ).wait_recv()

        each_peer(one)

    def arrived_z(buffer, send, recv):
        for d in range(1, n_feat):
            peer = feat_peer(d)
            remote(
                buffer.at[peer], buffer.at[peer], send.at[d], recv.at[peer], feat=peer
            ).wait_recv()

    UP_OUT, DOWN_OUT, LOW, HIGH = 0, 1, 2, 3

    def line_copies(c, up):
        way = 0 if up else 1
        out, into = (UP_OUT, LOW) if up else (DOWN_OUT, HIGH)
        peer = z + 1 if up else z - 1
        return (
            remote(
                codes.at[out, span(c)], codes.at[into, span(c)],
                line_send.at[way, 0, c], line_recv.at[way, 0, c], feat=peer,
            ),
            remote(
                scales.at[out, c], scales.at[into, c],
                line_send.at[way, 1, c], line_recv.at[way, 1, c], feat=peer,
            ),
        )

    def block_span(c, b):
        return pl.ds(pl.multiple_of(c * rows_chunk + b * BLK, BLK), BLK)

    def decode(slot, c, b):
        return codes[slot, block_span(c, b), :].astype(jnp.int32).astype(F32) * scales[
            slot, c, pl.ds(b, 1), :
        ]

    def post(c, up, values):
        slot = UP_OUT if up else DOWN_OUT
        for b in range(per_chunk):
            value = values(b)
            top = jnp.maximum(jnp.max(jnp.abs(value), axis=0, keepdims=True), 1e-30)
            code = jnp.round(value * (LEVELS / top)).astype(jnp.int32)
            codes[slot, block_span(c, b), :] = code.astype(jnp.int16)
            scales[slot, c, pl.ds(b, 1), :] = top * (1.0 / LEVELS)
        for copy in line_copies(c, up):
            copy.start()

    def relay(c, up):
        slot = LOW if up else HIGH
        for copy in line_copies(c, up):
            copy.wait_recv()

        @pl.when(outer if up else inner)
        def _():
            post(c, up, lambda b: proj[block_span(c, b), :] + decode(slot, c, b))

    def near(c):
        @pl.when(inner & lower)
        def _():
            relay(c, True)

        @pl.when(outer & jnp.logical_not(lower))
        def _():
            relay(c, False)

    def far(c):
        @pl.when(lower)
        def _():
            relay(c, False)

        @pl.when(jnp.logical_not(lower))
        def _():
            relay(c, True)

    def project(first, last):
        @pl.loop(first, last)
        def _(c):
            load(c).wait()
            proj[span(c), :] = dg(vis[span(c), :], factor_in[...], NN)

            @pl.when(z == 0)
            def _():
                post(c, True, lambda b: proj[block_span(c, b), :])

            @pl.when(z == n_feat - 1)
            def _():
                post(c, False, lambda b: proj[block_span(c, b), :])

    project(0, 4)
    arrived_z(gram_parts, gram_send, gram_recv)
    gram_mine[...] = jnp.sum(gram_parts[...], axis=0)
    gram_all[me] = gram_mine[...]
    for d in range(1, n_pat):
        gram_all_copy(d).start()
    project(4, 8)
    near(0)
    project(8, 12)
    near(1)
    project(12, chunks)

    arrived(weights_all, weight_send, weight_recv)
    arrived(gram_all, gram_all_send, gram_all_recv)

    lane = lax.broadcasted_iota(jnp.int32, (rank, rank), 1)
    sub = lax.broadcasted_iota(jnp.int32, (rank, rank), 0)
    identity = (lane == sub).astype(F32)
    all_rows = weights_all[...].reshape(n_pat * patients, rank)
    weight_gram = exact(all_rows, all_rows, TN)
    core_gram = exact(core[...], core[...], TN)
    feature_gram = jnp.concatenate([gram_all[q, 0] for q in range(owners)], axis=0)
    static_gram = jnp.concatenate([gram_all[q, 1] for q in range(owners)], axis=0)
    mats[0] = feature_gram * weight_gram + MU_RIDGE * identity
    mats[1] = core_gram * weight_gram + MU_RIDGE * identity
    mats[2] = core_gram * feature_gram + static_gram + MU_RIDGE * identity
    mats[3] = weight_gram + MU_RIDGE * identity
    which = lax.rem(me, quad)
    work[...] = mats[which]

    lane_row = lax.broadcasted_iota(jnp.int32, (1, rank), 1)
    sub_col = lax.broadcasted_iota(jnp.int32, (rank, 1), 0)

    def eliminate(k):
        whole = work[...]
        row = work[pl.ds(k, 1), :]
        pivot = jnp.sum(jnp.where(lane_row == k, row, 0.0), axis=1, keepdims=True)
        column = jnp.sum(jnp.where(lane == k, whole, 0.0), axis=1, keepdims=True)
        inverse = 1.0 / pivot
        scaled = jnp.where(lane_row == k, inverse, row * inverse)
        cleared = jnp.where((lane == k) | (sub == k), 0.0, whole)
        work[...] = cleared - jnp.where(sub_col == k, -1.0, column) * scaled

    starts, ends, lives = [], [], []
    position = jnp.int32(0)
    for k in range(patients):
        starts.append(position)
        lives.append(position + counts[k])
        position = position + ((counts[k] + (BLK - 1)) & (-BLK))
        ends.append(position)

    start_row = jnp.full((1, rank), rows, jnp.int32)
    live_row = jnp.zeros((1, rank), jnp.int32)
    patient_col = lax.broadcasted_iota(jnp.int32, (patients, 1), 0)
    start_col = jnp.full((patients, 1), rows, jnp.int32)
    end_col = jnp.zeros((patients, 1), jnp.int32)
    for k in range(patients):
        start_row = jnp.where(lane_row == k, starts[k], start_row)
        live_row = jnp.where(lane_row == k, lives[k], live_row)
        start_col = jnp.where(patient_col == k, starts[k], start_col)
        end_col = jnp.where(patient_col == k, ends[k], end_col)
    weight_pair = join(
        jnp.concatenate([weight[...], jnp.zeros((rank - patients, rank), F32)], axis=0)
    )
    chunk_row = lax.broadcasted_iota(jnp.int32, (rows_chunk, rank), 0)

    def finish(c):
        total[span(c), :] = proj[span(c), :]

        @pl.when(inner)
        def _():
            for b in range(per_chunk):
                total[block_span(c, b), :] += decode(LOW, c, b)

        @pl.when(outer)
        def _():
            for b in range(per_chunk):
                total[block_span(c, b), :] += decode(HIGH, c, b)

        at = chunk_row + c * rows_chunk
        live = jnp.where((at >= start_row) & (at < live_row), 1.0, 0.0).astype(BF16)
        by_row = halves_sum(dg(live, weight_pair, NN))
        wide = total[span(c), :] * by_row
        row_weights[span(c), :] = by_row
        wides[span(c), :] = wide
        for b in range(per_chunk):
            one = join(wide[b * BLK : (b + 1) * BLK])
            both = dg(one, one, TN)
            squares[c * per_chunk + b] = halves_sum(both[:rank] + both[rank:])

    lag = 2
    share = rank // chunks

    def eliminate_some(first):
        @pl.loop(0, share)
        def _(j):
            eliminate(first + j)

    @pl.loop(lag, chunks)
    def _(c):
        near(c)
        far(c - lag)
        finish(c - lag)
        eliminate_some((c - lag) * share)

    @pl.loop(chunks, chunks + lag)
    def _(c):
        far(c - lag)
        finish(c - lag)
        eliminate_some((c - lag) * share)

    def inv_peer(d):
        return lax.div(me, quad) * quad + lax.rem(me + d, quad)

    inverses[which] = work[...]

    def inv_copy(d):
        return remote(
            inverses.at[which], inverses.at[which], inv_send.at[d], inv_recv.at[which],
            pat=inv_peer(d),
        )

    for d in range(1, quad):
        inv_copy(d).start()

    most = MAXV // BLK
    for k in range(patients):
        first = lax.shift_right_logical(starts[k], 7)
        after = lax.shift_right_logical(ends[k], 7)
        square = squares[first]
        for i in range(1, most):
            keep = jnp.where(first + i < after, 1.0, 0.0).astype(F32)
            square = square + keep * squares[jnp.minimum(first + i, blocks - 1)]
        half = dot4(core[...], square)
        halves[k] = half
        gram = dot4_nt(half, core[...])
        trace = jnp.sum(jnp.sum(gram * identity, axis=1, keepdims=True), axis=0, keepdims=True)
        grams[k] = gram / trace
        factors[k] = identity / jnp.sqrt(trace)

    @pl.loop(0, NS_STEPS)
    def _(step):
        for k in range(patients):
            moment = grams[k]
            correction = twice(1.5 * identity - 0.5 * moment)
            both = jnp.concatenate([factors[k], moment], axis=0)
            both = halves_sum(dg(join(both), correction, NN))
            factors[k] = both[:rank]
            grams[k] = halves_sum(dg(join(both[rank:]), correction, NN))

    core_terms = jnp.zeros((rank, rank), F32)
    for k in range(patients):
        factor = factors[k]
        core_terms = core_terms + dot4_tn(factor, halves[k])
        mappers[k] = twice(dot4_tn(core[...], dot4(factor, core[...])))

    core_sum_own[...] = core_terms.reshape(owners, core_rows, rank)

    def core_z_copy(d):
        return remote(
            core_sum_own, core_used, core_z_send.at[d], core_z_recv.at[0], feat=feat_peer(d)
        )

    def patient_copy(d):
        return remote(
            patient_sum, patient_used, patient_send.at[d], patient_recv.at[0], feat=feat_peer(d)
        )

    @pl.when(z == source)
    def _():
        core_used[...] = core_sum_own[...]
        for d in range(1, n_feat):
            core_z_copy(d).start()

    group = 8
    group_rows = group * BLK

    def map_group(g, sums):
        for i in range(group):
            b = g * group + i
            at = b * BLK
            span_b = pl.ds(pl.multiple_of(at, BLK), BLK)
            owner = jnp.int32(0)
            for k in range(patients - 1):
                owner = owner + jnp.where(at >= ends[k], 1, 0)
            mapped = halves_sum(dg(join(wides[span_b, :]), mappers[owner], NN))
            products = mapped * total[span_b, :]
            updates[span_b, :] = (mapped * row_weights[span_b, :]).astype(BF16)
            member = jnp.where((at >= start_col) & (at < end_col), 1.0, 0.0).astype(F32)
            sums = sums + member * jnp.sum(products, axis=0, keepdims=True)
        return sums

    patient_sum[...] = lax.fori_loop(
        0, blocks // group, map_group, jnp.zeros((patients, rank), F32)
    )

    @pl.when(z == source)
    def _():
        patient_used[...] = patient_sum[...]
        for d in range(1, n_feat):
            patient_copy(d).start()

    for d in range(1, quad):
        peer = inv_peer(d)
        slot = lax.rem(me + d, quad)
        remote(
            inverses.at[slot], inverses.at[slot], inv_send.at[d], inv_recv.at[slot], pat=peer
        ).wait_recv()

    width = features // tiles
    per = n_pat // tiles

    def terms_copy(peer):
        return remote(
            terms_out.at[peer], terms_in.at[me], terms_send.at[peer], terms_recv.at[me], pat=peer
        )

    def core_copy(d):
        peer = pat_peer(d)
        return remote(
            core_used.at[lax.rem(peer, owners)], core_in.at[me], core_send.at[d],
            core_recv.at[me], pat=peer,
        )

    def some_tiles(first, last):
        @pl.loop(first, last)
        def _(s):
            tile = lax.rem(lax.div(me, per) + 1 + s, tiles)
            columns = pl.ds(pl.multiple_of(tile * width, width), width)
            acc = jnp.zeros((width, rank), F32)
            for g in range(blocks // group):
                acc = acc + dg(
                    vis[g * group_rows : (g + 1) * group_rows, columns],
                    updates[g * group_rows : (g + 1) * group_rows, :],
                    TN,
                )
            acc = solve(acc, mats[1], inverses[1]).astype(BF16)
            for j in range(per):
                peer = tile * per + j
                terms_out[peer] = acc[j * piece : (j + 1) * piece]

                @pl.when(peer != me)
                def _():
                    terms_copy(peer).start()

    some_tiles(0, tiles // 2)

    @pl.when(z != source)
    def _():
        core_z_copy(0).wait_recv()

    core_in[me] = core_used[mine]
    for d in range(1, n_pat):
        core_copy(d).start()

    some_tiles(tiles // 2, tiles)

    arrived(core_in, core_send, core_recv)
    terms_in[me] = terms_out[me]
    arrived(terms_in, terms_send, terms_recv)

    core_sum = jnp.sum(core_in[...], axis=0)
    coreg_out[...] = solve(core_sum, mats[0], inverses[0])
    terms_sum = jnp.sum(terms_in[...].astype(F32), axis=0)
    new_out[...] = terms_sum.astype(BF16)

    def new_copy(d):
        return remote(new_out, new_in.at[me], new_send.at[d], new_recv.at[me], pat=pat_peer(d))

    def coreg_copy(d):
        return remote(
            coreg_out, coreg_in.at[me], coreg_send.at[d], coreg_recv.at[me], pat=pat_peer(d)
        )

    for d in range(1, n_pat):
        new_copy(d).start()
        coreg_copy(d).start()
    new_in[me] = new_out[...]
    coreg_in[me] = coreg_out[...]

    @pl.when(z != source)
    def _():
        patient_copy(0).wait_recv()

    arrived_z(coupled_parts, coupled_send, coupled_recv)
    coupled = jnp.sum(coupled_parts[...], axis=0)
    patient_new[...] = solve(patient_used[...] + coupled, mats[2], inverses[2])
    arrived(static_all, static_send, static_recv)
    static_terms = exact(static_all[...].reshape(n_pat * patients, -1), all_rows, TN)
    static_new[...] = solve(static_terms, mats[3], inverses[3])

    arrived(coreg_in, coreg_send, coreg_recv)
    for q in range(owners):
        core_new[pl.ds(q * core_rows, core_rows), :] = coreg_in[q]
    arrived(new_in, new_send, new_recv)
    feature_new[...] = new_in[...].astype(F32).reshape(features, rank)

    for d in range(1, n_pat):
        weight_copy(d).wait_send()
        static_copy(d).wait_send()
        gram_all_copy(d).wait_send()
        core_copy(d).wait_send()
        new_copy(d).wait_send()
        coreg_copy(d).wait_send()
        terms_copy(pat_peer(d)).wait_send()
    for d in range(1, quad):
        inv_copy(d).wait_send()
    for d in range(1, n_feat):
        gram_copy(d).wait_send()
        coupled_copy(d).wait_send()

    @pl.when(z == source)
    def _():
        for d in range(1, n_feat):
            core_z_copy(d).wait_send()
            patient_copy(d).wait_send()

    @pl.loop(0, chunks)
    def _(c):
        @pl.when(outer)
        def _():
            for copy in line_copies(c, True):
                copy.wait_send()

        @pl.when(inner)
        def _():
            for copy in line_copies(c, False):
                copy.wait_send()


def local(n_pat, n_feat, visits, counts, weight, core, factor, static_data, static_factor):
    rows, features = visits.shape
    patients, rank = weight.shape
    columns = static_data.shape[1]
    chunks = 16
    tiles = min(n_pat, features // 128)
    core_rows = max(rank // n_pat, 16)
    owners = rank // core_rows
    piece = features // n_pat
    blocks = rows // BLK
    vmem, dma = pltpu.VMEM, pltpu.SemaphoreType.DMA
    scratch = [
        vmem((rows, features), BF16),
        vmem((rows, rank), F32),
        vmem((rows, rank), F32),
        vmem((4, rows, rank), jnp.int16),
        vmem((4, chunks, blocks // chunks, rank), F32),
        vmem((2, owners, core_rows, rank), F32),
        vmem((n_feat, 2, core_rows, rank), F32),
        vmem((2, core_rows, rank), F32),
        vmem((n_pat, 2, core_rows, rank), F32),
        vmem((patients, rank), F32),
        vmem((n_feat, patients, rank), F32),
        vmem((n_pat, patients, rank), F32),
        vmem((n_pat, patients, columns), F32),
        vmem((4, rank, rank), F32),
        vmem((rank, rank), F32),
        vmem((4, rank, rank), F32),
        vmem((rows, rank), F32),
        vmem((rows, rank), F32),
        vmem((blocks, rank, rank), F32),
        vmem((patients, rank, rank), F32),
        vmem((patients, rank, rank), F32),
        vmem((patients, rank, rank), F32),
        vmem((patients, 2 * rank, 2 * rank), BF16),
        vmem((rows, rank), BF16),
        vmem((patients, rank), F32),
        vmem((patients, rank), F32),
        vmem((owners, core_rows, rank), F32),
        vmem((owners, core_rows, rank), F32),
        vmem((n_pat, piece, rank), BF16),
        vmem((n_pat, piece, rank), BF16),
        vmem((n_pat, core_rows, rank), F32),
        vmem((piece, rank), BF16),
        vmem((n_pat, piece, rank), BF16),
        vmem((core_rows, rank), F32),
        vmem((n_pat, core_rows, rank), F32),
        dma((chunks,)),
        dma((2, 2, chunks)),
        dma((2, 2, chunks)),
    ]
    scratch += [dma((n_feat,))] * 8 + [dma((4,))] * 2 + [dma((n_pat,))] * 14
    space = pl.BlockSpec(memory_space=pltpu.VMEM)
    return pl.pallas_call(
        functools.partial(kernel, n_pat, n_feat, chunks, tiles),
        out_shape=(
            jax.ShapeDtypeStruct((rank, rank), F32),
            jax.ShapeDtypeStruct((features, rank), F32),
            jax.ShapeDtypeStruct((patients, rank), F32),
            jax.ShapeDtypeStruct((columns, rank), F32),
        ),
        in_specs=[
            pl.BlockSpec(memory_space=pltpu.SMEM),
            pl.BlockSpec(memory_space=pl.ANY),
            space, space, space, space, space,
        ],
        out_specs=(space, space, space, space),
        scratch_shapes=scratch,
        compiler_params=pltpu.CompilerParams(
            collective_id=0, has_side_effects=True, vmem_limit_bytes=62 * 1024 * 1024
        ),
        name="sweep",
    )(counts, visits, weight, core, factor, static_data, static_factor)


def solution(mesh):
    return jax.shard_map(
        functools.partial(local, mesh.shape["pat"], mesh.shape["feat"]),
        mesh=mesh,
        in_specs=(
            P("pat", "feat"),
            P("pat"),
            P("pat", None),
            P(),
            P("feat", None),
            P("pat", "feat"),
            P("feat", None),
        ),
        out_specs=(P(), P("feat", None), P("pat", None), P("feat", None)),
        check_vma=False,
    )
```

time: 188 us -> 96.9 us (0.52)
  Pallas kernels: 180 us -> 89.1 us
    pallas_call x1, Pallas kernels: 180 us -> 89.1 us  [local(): pl.pallas_call(functools.partial(kernel, n_pat, n_feat, chunks, tiles), o...]
where the time goes in v1:
time: 96.9 us; the launch traced here: 96.6 us
  Pallas kernels  89.1 us (92%)
  local copies, waits for them, and re-layouts  6.88 us (7%)
    pallas_call x1, Pallas kernels, local(): pl.pallas_call(functools.partial(kernel, n_pat, n_feat, chunks, tiles), o...  89.1 us
    unnamed x4, local copies, waits for them, and re-layouts  6.88 us

profile of v1, /device:TPU:1, one launch (start us, length us, event | category | flops | bytes accessed | tf_op | source)
XLA Modules:
  0.0 96.6 jit_solution(8221432406095714785)
XLA Ops:
  0.6 89.1 %sweep.1 = (f32[128,128]{1,0:T(8,128)}, f32[2048,128]{1,0:T(8,128)}, f32[8,128]{1,0:T(8,128)}, f32[1024,128]{1,0:T(8,128)}) custom-call(s32[8]{0:T(128)} %counts.1, bf16[4096,2048]{1,0:T(8,128)(2,1)} %visits.1, f32[8,128]{1,0:T(8,128)} %weight.1, f32[128,128]{1,0:T(8,128)} %core.1, bf16[2048,128]{1,0:T(8,128)(2,1)} %factor_in.1, ...), custom_call_target="tpu_custom_call" | custom-call | tf_op jit(solution)/shard_map/sweep/pallas_call | solution.py:667
  89.7 1.5 %copy.15 = f32[128,128]{1,0:T(8,128)} copy(f32[128,128]{1,0:T(8,128)} %get-tuple-element.8) | data formatting | bytes 131072
  91.2 2.3 %copy.16 = f32[2048,128]{1,0:T(8,128)} copy(f32[2048,128]{1,0:T(8,128)} %get-tuple-element.9) | data formatting | bytes 2097152
  93.5 1.3 %copy.17 = f32[8,128]{1,0:T(8,128)} copy(f32[8,128]{1,0:T(8,128)} %get-tuple-element.10) | data formatting | bytes 8192
  94.8 1.9 %copy.18 = f32[1024,128]{1,0:T(8,128)} copy(f32[1024,128]{1,0:T(8,128)} %get-tuple-element.11) | data formatting | bytes 1048576

commit v2 on v1

--- a/solution.py
+++ b/solution.py
@@ -60,6 +60,13 @@
     return halves_sum(dg(jnp.concatenate(split(a), axis=0), twice(b), TN))
 
 
+def thirds(x):
+    high = x.astype(BF16)
+    rest = x - high.astype(F32)
+    middle = rest.astype(BF16)
+    return high, middle, (rest - middle.astype(F32)).astype(BF16)
+
+
 def exact(a, b, dims=NN):
     return lax.dot_general(
         a, b, dims, precision=lax.Precision.HIGHEST, preferred_element_type=F32
@@ -78,7 +85,7 @@
     vis, proj, total, codes, scales,
     gram_own, gram_parts, gram_mine, gram_all, coupled_own, coupled_parts,
     weights_all, static_all,
-    mats, work, inverses, wides, row_weights, squares, grams, factors, halves, mappers, updates,
+    mats, work, inverses, wides, row_weights, squares, grams, factors, halves, mappers, updates, left,
     patient_sum, patient_used, core_sum_own, core_used,
     terms_out, terms_in, core_in, new_out, new_in, coreg_out, coreg_in,
     vis_sem, line_send, line_recv,
@@ -315,14 +322,27 @@
     sub_col = lax.broadcasted_iota(jnp.int32, (rank, 1), 0)
 
     def eliminate(k):
+        n = k + 1
         whole = work[...]
-        row = work[pl.ds(k, 1), :]
-        pivot = jnp.sum(jnp.where(lane_row == k, row, 0.0), axis=1, keepdims=True)
-        column = jnp.sum(jnp.where(lane == k, whole, 0.0), axis=1, keepdims=True)
-        inverse = 1.0 / pivot
-        scaled = jnp.where(lane_row == k, inverse, row * inverse)
-        cleared = jnp.where((lane == k) | (sub == k), 0.0, whole)
-        work[...] = cleared - jnp.where(sub_col == k, -1.0, column) * scaled
+        row_a = work[pl.ds(k, 1), :]
+        row_b = work[pl.ds(n, 1), :]
+
+        def pick(row, at):
+            return jnp.sum(jnp.where(lane_row == at, row, 0.0), axis=1, keepdims=True)
+
+        aa, ab, ba, bb = pick(row_a, k), pick(row_a, n), pick(row_b, k), pick(row_b, n)
+        column_a = jnp.sum(jnp.where(lane == k, whole, 0.0), axis=1, keepdims=True)
+        column_b = jnp.sum(jnp.where(lane == n, whole, 0.0), axis=1, keepdims=True)
+        inverse = 1.0 / (aa * bb - ab * ba)
+        row_a = jnp.where(lane_row == k, 1.0, jnp.where(lane_row == n, 0.0, row_a))
+        row_b = jnp.where(lane_row == n, 1.0, jnp.where(lane_row == k, 0.0, row_b))
+        scaled_a = (bb * inverse) * row_a - (ab * inverse) * row_b
+        scaled_b = (aa * inverse) * row_b - (ba * inverse) * row_a
+        pivots = (lane == k) | (sub == k) | (lane == n) | (sub == n)
+        cleared = jnp.where(pivots, 0.0, whole)
+        column_a = jnp.where(sub_col == k, -1.0, jnp.where(sub_col == n, 0.0, column_a))
+        column_b = jnp.where(sub_col == n, -1.0, jnp.where(sub_col == k, 0.0, column_b))
+        work[...] = cleared - column_a * scaled_a - column_b * scaled_b
 
     starts, ends, lives = [], [], []
     position = jnp.int32(0)
@@ -375,9 +395,9 @@
     share = rank // chunks
 
     def eliminate_some(first):
-        @pl.loop(0, share)
+        @pl.loop(0, share // 2)
         def _(j):
-            eliminate(first + j)
+            eliminate(first + 2 * j)
 
     @pl.loop(lag, chunks)
     def _(c):
@@ -407,35 +427,53 @@
         inv_copy(d).start()
 
     most = MAXV // BLK
-    for k in range(patients):
+    every = range(patients)
+    sums = []
+    for k in every:
         first = lax.shift_right_logical(starts[k], 7)
         after = lax.shift_right_logical(ends[k], 7)
         square = squares[first]
         for i in range(1, most):
             keep = jnp.where(first + i < after, 1.0, 0.0).astype(F32)
             square = square + keep * squares[jnp.minimum(first + i, blocks - 1)]
-        half = dot4(core[...], square)
-        halves[k] = half
-        gram = dot4_nt(half, core[...])
-        trace = jnp.sum(jnp.sum(gram * identity, axis=1, keepdims=True), axis=0, keepdims=True)
-        grams[k] = gram / trace
+        sums.append(square)
+    sums = [dot4(core[...], square) for square in sums]
+    for k in every:
+        halves[k] = sums[k]
+    products = [dot4_nt(half, core[...]) for half in sums]
+    for k in every:
+        trace = jnp.sum(
+            jnp.sum(products[k] * identity, axis=1, keepdims=True), axis=0, keepdims=True
+        )
+        grams[k] = products[k] / trace
         factors[k] = identity / jnp.sqrt(trace)
 
-    @pl.loop(0, NS_STEPS)
+    def corrections():
+        return [twice(1.5 * identity - 0.5 * grams[k]) for k in every]
+
+    @pl.loop(0, NS_STEPS - 1)
     def _(step):
-        for k in range(patients):
+        rights, firsts = [], []
+        for k in every:
             moment = grams[k]
-            correction = twice(1.5 * identity - 0.5 * moment)
+            right = twice(1.5 * identity - 0.5 * moment)
             both = jnp.concatenate([factors[k], moment], axis=0)
-            both = halves_sum(dg(join(both), correction, NN))
+            rights.append(right)
+            firsts.append(dg(join(both), right, NN))
+        for k in every:
+            both = halves_sum(firsts[k])
             factors[k] = both[:rank]
-            grams[k] = halves_sum(dg(join(both[rank:]), correction, NN))
-
-    core_terms = jnp.zeros((rank, rank), F32)
-    for k in range(patients):
-        factor = factors[k]
-        core_terms = core_terms + dot4_tn(factor, halves[k])
-        mappers[k] = twice(dot4_tn(core[...], dot4(factor, core[...])))
+            grams[k] = halves_sum(dg(join(both[rank:]), rights[k], NN))
+
+    rights = corrections()
+    lasts = [halves_sum(dg(join(factors[k]), rights[k], NN)) for k in every]
+    mapped_core = [dot4(factor, core[...]) for factor in lasts]
+    for k in every:
+        mappers[k] = twice(dot4_tn(core[...], mapped_core[k]))
+    parts = [dot4_tn(lasts[k], halves[k]) for k in every]
+    core_terms = parts[0]
+    for k in range(1, patients):
+        core_terms = core_terms + parts[k]
 
     core_sum_own[...] = core_terms.reshape(owners, core_rows, rank)
 
@@ -456,19 +494,22 @@
             core_z_copy(d).start()
 
     group = 8
-    group_rows = group * BLK
 
     def map_group(g, sums):
+        raw = []
         for i in range(group):
-            b = g * group + i
-            at = b * BLK
-            span_b = pl.ds(pl.multiple_of(at, BLK), BLK)
+            at = (g * group + i) * BLK
             owner = jnp.int32(0)
             for k in range(patients - 1):
                 owner = owner + jnp.where(at >= ends[k], 1, 0)
-            mapped = halves_sum(dg(join(wides[span_b, :]), mappers[owner], NN))
+            wide = wides[pl.ds(pl.multiple_of(at, BLK), BLK), :]
+            raw.append(dg(join(wide), mappers[owner], NN))
+        for i in range(group):
+            at = (g * group + i) * BLK
+            span_b = pl.ds(pl.multiple_of(at, BLK), BLK)
+            mapped = halves_sum(raw[i])
             products = mapped * total[span_b, :]
-            updates[span_b, :] = (mapped * row_weights[span_b, :]).astype(BF16)
+            updates[:, span_b] = jnp.transpose(mapped * row_weights[span_b, :]).astype(BF16)
             member = jnp.where((at >= start_col) & (at < end_col), 1.0, 0.0).astype(F32)
             sums = sums + member * jnp.sum(products, axis=0, keepdims=True)
         return sums
@@ -510,14 +551,9 @@
         def _(s):
             tile = lax.rem(lax.div(me, per) + 1 + s, tiles)
             columns = pl.ds(pl.multiple_of(tile * width, width), width)
-            acc = jnp.zeros((width, rank), F32)
-            for g in range(blocks // group):
-                acc = acc + dg(
-                    vis[g * group_rows : (g + 1) * group_rows, columns],
-                    updates[g * group_rows : (g + 1) * group_rows, :],
-                    TN,
-                )
-            acc = solve(acc, mats[1], inverses[1]).astype(BF16)
+            high, middle, low = thirds(dg(updates[...], vis[:, columns], NN))
+            right = jnp.concatenate([high, high, middle, middle, low, high], axis=0)
+            acc = jnp.transpose(dg(left[...], right, NN)).astype(BF16)
             for j in range(per):
                 peer = tile * per + j
                 terms_out[peer] = acc[j * piece : (j + 1) * piece]
@@ -525,6 +561,9 @@
                 @pl.when(peer != me)
                 def _():
                     terms_copy(peer).start()
+
+    high, middle, low = thirds(inverses[1])
+    left[...] = jnp.concatenate([high, middle, high, middle, high, low], axis=1)
 
     some_tiles(0, tiles // 2)
 
@@ -616,7 +655,7 @@
     patients, rank = weight.shape
     columns = static_data.shape[1]
     chunks = 16
-    tiles = min(n_pat, features // 128)
+    tiles = max(features // 512, 1)
     core_rows = max(rank // n_pat, 16)
     owners = rank // core_rows
     piece = features // n_pat
@@ -646,7 +685,8 @@
         vmem((patients, rank, rank), F32),
         vmem((patients, rank, rank), F32),
         vmem((patients, 2 * rank, 2 * rank), BF16),
-        vmem((rows, rank), BF16),
+        vmem((rank, rows), BF16),
+        vmem((rank, 6 * rank), BF16),
         vmem((patients, rank), F32),
         vmem((patients, rank), F32),
         vmem((owners, core_rows, rank), F32),

time: 96.9 us -> 81 us (0.84)
  Pallas kernels: 89.1 us -> 73.1 us
    pallas_call x1, Pallas kernels: 89.1 us -> 73.1 us  [local(): pl.pallas_call(functools.partial(kernel, n_pat, n_feat, chunks, tiles), o...]
where the time goes in v2:
time: 81 us; the launch traced here: 80.7 us
  Pallas kernels  73.1 us (90%)
  local copies, waits for them, and re-layouts  6.88 us (8%)
    pallas_call x1, Pallas kernels, local(): pl.pallas_call(functools.partial(kernel, n_pat, n_feat, chunks, tiles), o...  73.1 us
    unnamed x4, local copies, waits for them, and re-layouts  6.88 us

profile of v2, /device:TPU:1, one launch (start us, length us, event | category | flops | bytes accessed | tf_op | source)
XLA Modules:
  0.0 80.7 jit_solution(8114834301864088432)
XLA Ops:
  0.6 73.1 %sweep.1 = (f32[128,128]{1,0:T(8,128)}, f32[2048,128]{1,0:T(8,128)}, f32[8,128]{1,0:T(8,128)}, f32[1024,128]{1,0:T(8,128)}) custom-call(s32[8]{0:T(128)} %counts.1, bf16[4096,2048]{1,0:T(8,128)(2,1)} %visits.1, f32[8,128]{1,0:T(8,128)} %weight.1, f32[128,128]{1,0:T(8,128)} %core.1, bf16[2048,128]{1,0:T(8,128)(2,1)} %factor_in.1, ...), custom_call_target="tpu_custom_call" | custom-call | tf_op jit(solution)/shard_map/sweep/pallas_call | solution.py:707
  73.8 1.5 %copy.15 = f32[128,128]{1,0:T(8,128)} copy(f32[128,128]{1,0:T(8,128)} %get-tuple-element.8) | data formatting | bytes 131072
  75.3 2.3 %copy.16 = f32[2048,128]{1,0:T(8,128)} copy(f32[2048,128]{1,0:T(8,128)} %get-tuple-element.9) | data formatting | bytes 2097152
  77.5 1.3 %copy.17 = f32[8,128]{1,0:T(8,128)} copy(f32[8,128]{1,0:T(8,128)} %get-tuple-element.10) | data formatting | bytes 8192
  78.8 1.9 %copy.18 = f32[1024,128]{1,0:T(8,128)} copy(f32[1024,128]{1,0:T(8,128)} %get-tuple-element.11) | data formatting | bytes 1048576

commit v3 on v2

--- a/solution.py
+++ b/solution.py
@@ -80,8 +80,9 @@
 
 def kernel(
     n_pat, n_feat, chunks, tiles,
-    counts, visits, weight, core, factor_in, static_data, static_factor,
+    counts, visits, weight_hbm, core_hbm, factor_hbm, data_hbm, static_hbm,
     core_new, feature_new, patient_new, static_new,
+    weight, core, factor_in, static_data, static_factor, input_sem,
     vis, proj, total, codes, scales,
     gram_own, gram_parts, gram_mine, gram_all, coupled_own, coupled_parts,
     weights_all, static_all,
@@ -131,6 +132,18 @@
     def feat_peer(d):
         return lax.rem(z + d, n_feat)
 
+    inputs = [
+        pltpu.make_async_copy(source_ref, held, input_sem.at[i])
+        for i, (source_ref, held) in enumerate(
+            (
+                (factor_hbm, factor_in), (static_hbm, static_factor), (data_hbm, static_data),
+                (weight_hbm, weight), (core_hbm, core),
+            )
+        )
+    ]
+    for copy in inputs:
+        copy.start()
+
     @pl.loop(0, chunks)
     def _(c):
         load(c).start()
@@ -145,6 +158,8 @@
             barrier, inc=1, device_id={"feat": feat_peer(d)}, device_id_type=MESH
         )
 
+    for copy in inputs:
+        copy.wait()
     weights_all[me] = weight[...]
     static_all[me] = static_data[...].astype(F32)
     gram_own[0] = dg(factor_in[...], factor_in[...], TN).reshape(owners, core_rows, rank)
@@ -275,30 +290,34 @@
             relay(c, True)
 
     def project(first, last):
-        @pl.loop(first, last)
-        def _(c):
-            load(c).wait()
-            proj[span(c), :] = dg(vis[span(c), :], factor_in[...], NN)
+        @pl.loop(first // 2, last // 2)
+        def _(p):
+            load(2 * p).wait()
+            load(2 * p + 1).wait()
+            both = pl.ds(pl.multiple_of(p * 2 * rows_chunk, rows_chunk), 2 * rows_chunk)
+            proj[both, :] = dg(vis[both, :], factor_in[...], NN)
 
             @pl.when(z == 0)
             def _():
-                post(c, True, lambda b: proj[block_span(c, b), :])
+                for i in range(2):
+                    post(2 * p + i, True, lambda b, i=i: proj[block_span(2 * p + i, b), :])
 
             @pl.when(z == n_feat - 1)
             def _():
-                post(c, False, lambda b: proj[block_span(c, b), :])
-
-    project(0, 4)
+                for i in range(2):
+                    post(2 * p + i, False, lambda b, i=i: proj[block_span(2 * p + i, b), :])
+
+    project(0, 6)
     arrived_z(gram_parts, gram_send, gram_recv)
     gram_mine[...] = jnp.sum(gram_parts[...], axis=0)
     gram_all[me] = gram_mine[...]
     for d in range(1, n_pat):
         gram_all_copy(d).start()
-    project(4, 8)
+    project(6, 10)
     near(0)
-    project(8, 12)
+    project(10, 14)
     near(1)
-    project(12, chunks)
+    project(14, chunks)
 
     arrived(weights_all, weight_send, weight_recv)
     arrived(gram_all, gram_all_send, gram_all_recv)
@@ -650,6 +669,16 @@
                 copy.wait_send()
 
 
+def deliver(*refs):
+    copies = [
+        pltpu.make_async_copy(refs[i], refs[4 + i], refs[8].at[i]) for i in range(4)
+    ]
+    for copy in copies:
+        copy.start()
+    for copy in copies:
+        copy.wait()
+
+
 def local(n_pat, n_feat, visits, counts, weight, core, factor, static_data, static_factor):
     rows, features = visits.shape
     patients, rank = weight.shape
@@ -662,6 +691,12 @@
     blocks = rows // BLK
     vmem, dma = pltpu.VMEM, pltpu.SemaphoreType.DMA
     scratch = [
+        vmem((patients, rank), F32),
+        vmem((rank, rank), F32),
+        vmem((features, rank), BF16),
+        vmem((patients, columns), BF16),
+        vmem((columns, rank), BF16),
+        dma((5,)),
         vmem((rows, features), BF16),
         vmem((rows, rank), F32),
         vmem((rows, rank), F32),
@@ -703,27 +738,29 @@
         dma((2, 2, chunks)),
     ]
     scratch += [dma((n_feat,))] * 8 + [dma((4,))] * 2 + [dma((n_pat,))] * 14
-    space = pl.BlockSpec(memory_space=pltpu.VMEM)
-    return pl.pallas_call(
+    anywhere = pl.BlockSpec(memory_space=pl.ANY)
+    near_by = pl.BlockSpec(memory_space=pltpu.VMEM)
+    shapes = ((rank, rank), (features, rank), (patients, rank), (columns, rank))
+    results = pl.pallas_call(
         functools.partial(kernel, n_pat, n_feat, chunks, tiles),
-        out_shape=(
-            jax.ShapeDtypeStruct((rank, rank), F32),
-            jax.ShapeDtypeStruct((features, rank), F32),
-            jax.ShapeDtypeStruct((patients, rank), F32),
-            jax.ShapeDtypeStruct((columns, rank), F32),
-        ),
-        in_specs=[
-            pl.BlockSpec(memory_space=pltpu.SMEM),
-            pl.BlockSpec(memory_space=pl.ANY),
-            space, space, space, space, space,
-        ],
-        out_specs=(space, space, space, space),
+        out_shape=tuple(vmem(shape, F32) for shape in shapes),
+        in_specs=[pl.BlockSpec(memory_space=pltpu.SMEM)] + [anywhere] * 6,
+        out_specs=(near_by,) * 4,
         scratch_shapes=scratch,
         compiler_params=pltpu.CompilerParams(
-            collective_id=0, has_side_effects=True, vmem_limit_bytes=62 * 1024 * 1024
+            collective_id=0, has_side_effects=True, vmem_limit_bytes=56 * 1024 * 1024
         ),
         name="sweep",
     )(counts, visits, weight, core, factor, static_data, static_factor)
+    results = [pltpu.with_memory_space_constraint(x, pltpu.VMEM) for x in results]
+    return pl.pallas_call(
+        deliver,
+        out_shape=tuple(jax.ShapeDtypeStruct(shape, F32) for shape in shapes),
+        in_specs=[near_by] * 4,
+        out_specs=(anywhere,) * 4,
+        scratch_shapes=[dma((4,))],
+        name="deliver",
+    )(*results)
 
 
 def solution(mesh):

time: 81 us -> 72.8 us (0.90)
  local copies, waits for them, and re-layouts: 6.88 us -> 0 us
  Pallas kernels: 73.1 us -> 72 us
    unnamed x4 -> x0, local copies, waits for them, and re-layouts: 6.88 us -> none
    pallas_call x1, Pallas kernels: 73.1 us -> 70.8 us  [local(): pl.pallas_call(functools.partial(kernel, n_pat, n_feat, chunks, tiles), o...]
    pallas_call x0 -> x1, Pallas kernels: none -> 1.2 us  [local(): pl.pallas_call(deliver, out_shape=tuple((jax.ShapeDtypeStruct(shape, F32)...]
where the time goes in v3:
time: 72.8 us; the launch traced here: 72.6 us
  Pallas kernels  72 us (99%)
    pallas_call x1, Pallas kernels, local(): pl.pallas_call(functools.partial(kernel, n_pat, n_feat, chunks, tiles), o...  70.8 us

profile of v3, /device:TPU:1, one launch (start us, length us, event | category | flops | bytes accessed | tf_op | source)
XLA Modules:
  0.0 72.6 jit_solution(4660730845322677473)
XLA Ops:
  0.6 70.8 %sweep.1 = (f32[128,128]{1,0:T(8,128)S(1)}, f32[2048,128]{1,0:T(8,128)S(1)}, f32[8,128]{1,0:T(8,128)S(1)}, f32[1024,128]{1,0:T(8,128)S(1)}) custom-call(s32[8]{0:T(128)} %counts.1, bf16[4096,2048]{1,0:T(8,128)(2,1)} %visits.1, f32[8,128]{1,0:T(8,128)} %weight_hbm.1, f32[128,128]{1,0:T(8,128)} %core_hbm.1, bf16[2048,128]{1,0:T(8,128)(2,1)} %factor_hbm.1, ...), custom_call_target="tpu_custom_call" | custom-call | tf_op jit(solution)/shard_map/sweep/pallas_call | solution.py:744
  71.4 1.2 %deliver.1 = (f32[128,128]{1,0:T(8,128)}, f32[2048,128]{1,0:T(8,128)}, f32[8,128]{1,0:T(8,128)}, f32[1024,128]{1,0:T(8,128)}) custom-call(f32[128,128]{1,0:T(8,128)S(1)} %get-tuple-element.8.refs_0_, f32[2048,128]{1,0:T(8,128)S(1)} %get-tuple-element.9.refs_1_, f32[8,128]{1,0:T(8,128)S(1)} %get-tuple-element.10.refs_2_, ...), custom_call_target="tpu_custom_call" | custom-call | tf_op jit(solution)/shard_map/deliver/pallas_call | solution.py:756

commit v4 on v3

--- a/solution.py
+++ b/solution.py
@@ -94,7 +94,7 @@
     core_z_send, core_z_recv, inv_send, inv_recv,
     gram_all_send, gram_all_recv, weight_send, weight_recv, static_send, static_recv,
     terms_send, terms_recv, core_send, core_recv,
-    new_send, new_recv, coreg_send, coreg_recv,
+    new_send, new_recv, coreg_send, coreg_recv, pass_send,
 ):
     me = lax.axis_index("pat")
     z = lax.axis_index("feat")
@@ -307,36 +307,9 @@
                 for i in range(2):
                     post(2 * p + i, False, lambda b, i=i: proj[block_span(2 * p + i, b), :])
 
-    project(0, 6)
-    arrived_z(gram_parts, gram_send, gram_recv)
-    gram_mine[...] = jnp.sum(gram_parts[...], axis=0)
-    gram_all[me] = gram_mine[...]
-    for d in range(1, n_pat):
-        gram_all_copy(d).start()
-    project(6, 10)
-    near(0)
-    project(10, 14)
-    near(1)
-    project(14, chunks)
-
-    arrived(weights_all, weight_send, weight_recv)
-    arrived(gram_all, gram_all_send, gram_all_recv)
-
     lane = lax.broadcasted_iota(jnp.int32, (rank, rank), 1)
     sub = lax.broadcasted_iota(jnp.int32, (rank, rank), 0)
     identity = (lane == sub).astype(F32)
-    all_rows = weights_all[...].reshape(n_pat * patients, rank)
-    weight_gram = exact(all_rows, all_rows, TN)
-    core_gram = exact(core[...], core[...], TN)
-    feature_gram = jnp.concatenate([gram_all[q, 0] for q in range(owners)], axis=0)
-    static_gram = jnp.concatenate([gram_all[q, 1] for q in range(owners)], axis=0)
-    mats[0] = feature_gram * weight_gram + MU_RIDGE * identity
-    mats[1] = core_gram * weight_gram + MU_RIDGE * identity
-    mats[2] = core_gram * feature_gram + static_gram + MU_RIDGE * identity
-    mats[3] = weight_gram + MU_RIDGE * identity
-    which = lax.rem(me, quad)
-    work[...] = mats[which]
-
     lane_row = lax.broadcasted_iota(jnp.int32, (1, rank), 1)
     sub_col = lax.broadcasted_iota(jnp.int32, (rank, 1), 0)
 
@@ -411,25 +384,65 @@
             squares[c * per_chunk + b] = halves_sum(both[:rank] + both[rank:])
 
     lag = 2
-    share = rank // chunks
-
-    def eliminate_some(first):
-        @pl.loop(0, share // 2)
+    early = 3
+    pairs = rank // 2
+    steps = chunks - lag - early - 1
+    share = pairs // steps
+
+    def eliminate_some(first, count):
+        @pl.loop(0, count)
         def _(j):
-            eliminate(first + 2 * j)
-
-    @pl.loop(lag, chunks)
+            eliminate(2 * (first + j))
+
+    project(0, 10)
+    near(0)
+    project(10, 12)
+    arrived_z(gram_parts, gram_send, gram_recv)
+    gram_mine[...] = jnp.sum(gram_parts[...], axis=0)
+    gram_all[me] = gram_mine[...]
+    for d in range(1, n_pat):
+        gram_all_copy(d).start()
+    project(12, 14)
+    near(1)
+    project(14, chunks)
+
+    @pl.loop(lag, lag + early)
     def _(c):
         near(c)
         far(c - lag)
         finish(c - lag)
-        eliminate_some((c - lag) * share)
+
+    arrived(weights_all, weight_send, weight_recv)
+    arrived(gram_all, gram_all_send, gram_all_recv)
+
+    all_rows = weights_all[...].reshape(n_pat * patients, rank)
+    weight_gram = exact(all_rows, all_rows, TN)
+    core_gram = exact(core[...], core[...], TN)
+    feature_gram = jnp.concatenate([gram_all[q, 0] for q in range(owners)], axis=0)
+    static_gram = jnp.concatenate([gram_all[q, 1] for q in range(owners)], axis=0)
+    mats[0] = feature_gram * weight_gram + MU_RIDGE * identity
+    mats[1] = core_gram * weight_gram + MU_RIDGE * identity
+    mats[2] = core_gram * feature_gram + static_gram + MU_RIDGE * identity
+    mats[3] = weight_gram + MU_RIDGE * identity
+    which = lax.rem(me, quad)
+    work[...] = mats[which]
+
+    @pl.loop(lag + early, chunks - 1)
+    def _(c):
+        near(c)
+        far(c - lag)
+        finish(c - lag)
+        eliminate_some((c - lag - early) * share, share)
+
+    near(chunks - 1)
+    far(chunks - 1 - lag)
+    finish(chunks - 1 - lag)
+    eliminate_some(steps * share, pairs - steps * share)
 
     @pl.loop(chunks, chunks + lag)
     def _(c):
         far(c - lag)
         finish(c - lag)
-        eliminate_some((c - lag) * share)
 
     def inv_peer(d):
         return lax.div(me, quad) * quad + lax.rem(me + d, quad)
@@ -596,29 +609,6 @@
 
     some_tiles(tiles // 2, tiles)
 
-    arrived(core_in, core_send, core_recv)
-    terms_in[me] = terms_out[me]
-    arrived(terms_in, terms_send, terms_recv)
-
-    core_sum = jnp.sum(core_in[...], axis=0)
-    coreg_out[...] = solve(core_sum, mats[0], inverses[0])
-    terms_sum = jnp.sum(terms_in[...].astype(F32), axis=0)
-    new_out[...] = terms_sum.astype(BF16)
-
-    def new_copy(d):
-        return remote(new_out, new_in.at[me], new_send.at[d], new_recv.at[me], pat=pat_peer(d))
-
-    def coreg_copy(d):
-        return remote(
-            coreg_out, coreg_in.at[me], coreg_send.at[d], coreg_recv.at[me], pat=pat_peer(d)
-        )
-
-    for d in range(1, n_pat):
-        new_copy(d).start()
-        coreg_copy(d).start()
-    new_in[me] = new_out[...]
-    coreg_in[me] = coreg_out[...]
-
     @pl.when(z != source)
     def _():
         patient_copy(0).wait_recv()
@@ -630,10 +620,59 @@
     static_terms = exact(static_all[...].reshape(n_pat * patients, -1), all_rows, TN)
     static_new[...] = solve(static_terms, mats[3], inverses[3])
 
+    arrived(core_in, core_send, core_recv)
+    terms_in[me] = terms_out[me]
+    arrived(terms_in, terms_send, terms_recv)
+
+    core_sum = jnp.sum(core_in[...], axis=0)
+    coreg_out[...] = solve(core_sum, mats[0], inverses[0])
+    terms_sum = jnp.sum(terms_in[...].astype(F32), axis=0)
+    new_out[...] = terms_sum.astype(BF16)
+
+    partner = me + 1 - 2 * lax.rem(me, 2)
+
+    def same_core(j):
+        return lax.rem(me + 2 * j, n_pat)
+
+    def new_copy(j):
+        return remote(
+            new_out, new_in.at[me], new_send.at[j], new_recv.at[me],
+            pat=same_core(j) if j else partner,
+        )
+
+    def pass_copy(j):
+        held = same_core(j)
+        return remote(
+            new_in.at[held], new_in.at[held], pass_send.at[j], new_recv.at[held], pat=partner
+        )
+
+    def coreg_copy(d):
+        return remote(
+            coreg_out, coreg_in.at[me], coreg_send.at[d], coreg_recv.at[me], pat=pat_peer(d)
+        )
+
+    for j in range(1, n_pat // 2):
+        new_copy(j).start()
+    new_copy(0).start()
+    for d in range(1, n_pat):
+        coreg_copy(d).start()
+    new_in[me] = new_out[...]
+    coreg_in[me] = coreg_out[...]
+
+    def landed(held):
+        remote(
+            new_in.at[held], new_in.at[held], pass_send.at[0], new_recv.at[held], pat=partner
+        ).wait_recv()
+
+    for j in range(1, n_pat // 2):
+        landed(same_core(j))
+        pass_copy(j).start()
     arrived(coreg_in, coreg_send, coreg_recv)
     for q in range(owners):
         core_new[pl.ds(q * core_rows, core_rows), :] = coreg_in[q]
-    arrived(new_in, new_send, new_recv)
+    landed(partner)
+    for j in range(1, n_pat // 2):
+        landed(lax.rem(partner + 2 * j, n_pat))
     feature_new[...] = new_in[...].astype(F32).reshape(features, rank)
 
     for d in range(1, n_pat):
@@ -641,11 +680,14 @@
         static_copy(d).wait_send()
         gram_all_copy(d).wait_send()
         core_copy(d).wait_send()
-        new_copy(d).wait_send()
         coreg_copy(d).wait_send()
         terms_copy(pat_peer(d)).wait_send()
     for d in range(1, quad):
         inv_copy(d).wait_send()
+    for j in range(n_pat // 2):
+        new_copy(j).wait_send()
+    for j in range(1, n_pat // 2):
+        pass_copy(j).wait_send()
     for d in range(1, n_feat):
         gram_copy(d).wait_send()
         coupled_copy(d).wait_send()
@@ -737,7 +779,7 @@
         dma((2, 2, chunks)),
         dma((2, 2, chunks)),
     ]
-    scratch += [dma((n_feat,))] * 8 + [dma((4,))] * 2 + [dma((n_pat,))] * 14
+    scratch += [dma((n_feat,))] * 8 + [dma((4,))] * 2 + [dma((n_pat,))] * 15
     anywhere = pl.BlockSpec(memory_space=pl.ANY)
     near_by = pl.BlockSpec(memory_space=pltpu.VMEM)
     shapes = ((rank, rank), (features, rank), (patients, rank), (columns, rank))

time: 72.8 us -> 71.9 us (0.988)
  Pallas kernels: 72 us -> 71 us
    pallas_call x1, Pallas kernels: 70.8 us -> 69.8 us  [local(): pl.pallas_call(functools.partial(kernel, n_pat, n_feat, chunks, tiles), o...]
where the time goes in v4:
time: 71.9 us; the launch traced here: 71.8 us
  Pallas kernels  71 us (99%)
  between operations  0.8 us (1%)
    pallas_call x1, Pallas kernels, local(): pl.pallas_call(functools.partial(kernel, n_pat, n_feat, chunks, tiles), o...  69.8 us

profile of v4, /device:TPU:1, one launch (start us, length us, event | category | flops | bytes accessed | tf_op | source)
XLA Modules:
  0.0 71.8 jit_solution(4621650390931090303)
XLA Ops:
  0.6 69.8 %sweep.1 = (f32[128,128]{1,0:T(8,128)S(1)}, f32[2048,128]{1,0:T(8,128)S(1)}, f32[8,128]{1,0:T(8,128)S(1)}, f32[1024,128]{1,0:T(8,128)S(1)}) custom-call(s32[8]{0:T(128)} %counts.1, bf16[4096,2048]{1,0:T(8,128)(2,1)} %visits.1, f32[8,128]{1,0:T(8,128)} %weight_hbm.1, f32[128,128]{1,0:T(8,128)} %core_hbm.1, bf16[2048,128]{1,0:T(8,128)(2,1)} %factor_hbm.1, ...), custom_call_target="tpu_custom_call" | custom-call | tf_op jit(solution)/shard_map/sweep/pallas_call | solution.py:786
  70.4 1.2 %deliver.1 = (f32[128,128]{1,0:T(8,128)}, f32[2048,128]{1,0:T(8,128)}, f32[8,128]{1,0:T(8,128)}, f32[1024,128]{1,0:T(8,128)}) custom-call(f32[128,128]{1,0:T(8,128)S(1)} %get-tuple-element.8.refs_0_, f32[2048,128]{1,0:T(8,128)S(1)} %get-tuple-element.9.refs_1_, f32[8,128]{1,0:T(8,128)S(1)} %get-tuple-element.10.refs_2_, ...), custom_call_target="tpu_custom_call" | custom-call | tf_op jit(solution)/shard_map/deliver/pallas_call | solution.py:798
